TPU v7x, 32 devices: a whole 2x2x4 slice. The times are simulated.
32 devices in a mesh: group: 2 (over y), ctx: 4 (over z), head: 4 (over x, core).
Axes of the slice: x: 2, y: 2, z: 4, core: 2. Of those that a mesh axis runs over, the one named last changes fastest.
Arguments:
- head_input: bfloat16 [4096, 8192], P(('group', 'ctx'), 'head'), parts along dimension 0, may hold values from -6 to 6
- gate_input: bfloat16 [4096, 8192], P(('group', 'ctx'), 'head'), parts along dimension 0, may hold values from -40 to 40
- input_map: bfloat16 [4096, 2048], P(('group', 'ctx'), 'head'), parts along dimension 0, may hold values from -4 to 4
- output_map: bfloat16 [4096, 2048], P(('group', 'ctx'), 'head'), parts along dimension 0, may hold values from -4 to 4
- step_size: float32 [128, 4096], P('head', ('group', 'ctx')), parts along dimension 1, may hold values from 0.1 to 0.4
- decays: float32 [128, 4096], P('head', ('group', 'ctx')), parts along dimension 1, may hold values from 0.45 to 1
- bypass_scale: float32 [128], P('head'), may hold values from 1 to 4
- norm_gain: bfloat16 [8192], P('head'), may hold values from 0.099609375 to 1.8984375
- out_weight: bfloat16 [8192, 4096], P('head', 'ctx'), may hold values from -0.0625 to 0.0625
Outputs:
- layer_out: bfloat16 [4096, 4096], P(('group', 'ctx', 'head')), parts along dimension 0
There are 2 independent parts, one for each index of `group`. A program takes and returns all parts, laid end to end along the dimension named above; an argument that names none is the same for every part. Nothing has to cross between parts.
All inputs are finite; a program needn't handle non-finite values.
Results may differ from a plain program's by a relative error of at most 0.014.
Values may be sent and summed in bfloat16 or wider, within the bound.
A program may use at most 128 MiB of HBM per device.

v0:
```python
import jax
import jax.numpy as jnp
from jax import lax
from jax.sharding import PartitionSpec as P

HEADP = 64
STATE = 256
STRETCH = 128


def carried_in(shard, axis, combine, identity):
    size, position = (lax.axis_size(axis), lax.axis_index(axis))
    everything = jax.tree.map(
        lambda part, kind: lax.all_gather(part.astype(kind), axis),
        shard,
        (jnp.bfloat16, jnp.bfloat16),
    )
    start = jax.tree.map(
        lambda part, zero: jnp.broadcast_to(jnp.asarray(zero, part.dtype), part.shape),
        shard,
        identity,
    )

    def lap(k, before):
        reached = k < position
        new = combine(
            before, jax.tree.map(lambda part, own: part[k].astype(own.dtype), everything, shard)
        )
        return jax.tree.map(lambda a, b: jnp.where(reached, a, b), new, before)

    return lax.fori_loop(0, size, lap, start)


def block_term_values(inputs, in_maps, out_maps, steps, decays):
    count, length, groups, per_group, channels = inputs.shape
    ramps = jnp.cumsum(jnp.log(decays), axis=-1)
    rows = lax.broadcasted_iota(jnp.int32, (length, length), 0)
    cols = lax.broadcasted_iota(jnp.int32, (length, length), 1)
    lower = rows >= cols
    spread = ramps[:, :, :, None] - ramps[:, :, None, :]
    within_decay = jnp.where(lower, jnp.exp(jnp.where(lower, spread, 0.0)), 0.0)
    scores = jnp.einsum("kqgn,ksgn->kgqs", out_maps, in_maps, preferred_element_type=jnp.float32)
    mixing = within_decay.reshape(count, groups, per_group, length, length) * scores[:, :, None]
    mixing = mixing * steps.reshape(count, groups, per_group, 1, length)
    mixing = mixing.astype(jnp.bfloat16)
    within = jnp.einsum("kgjqs,ksgjp->kqgjp", mixing, inputs, preferred_element_type=jnp.float32)
    tails = jnp.exp(ramps[:, :, -1:] - ramps) * steps
    tails = jnp.transpose(tails.reshape(count, groups, per_group, length), (0, 3, 1, 2))[..., None]
    weighted = (inputs.astype(jnp.float32) * tails).astype(jnp.bfloat16)
    block_state = jnp.einsum(
        "ksgjp,ksgn->kgjpn", weighted, in_maps, preferred_element_type=jnp.float32
    )
    accumulated_sums_list = jnp.exp(ramps[:, :, -1]).reshape(count, groups, per_group)
    entry = jnp.transpose(jnp.exp(ramps).reshape(count, groups, per_group, length), (0, 3, 1, 2))[
        ..., None
    ]
    return (within, block_state, accumulated_sums_list, entry)


def join_states(earlier, later):
    early_decay, early_state = earlier
    late_decay, late_state = later
    return (early_decay * late_decay, late_decay[..., None, None] * early_state + late_state)


def shards(
    head_input,
    gate_input,
    input_map,
    output_map,
    step_size,
    decays,
    bypass_scale,
    norm_gain,
    out_weight,
):
    tok_rows, width = head_input.shape
    heads = step_size.shape[0]
    groups = input_map.shape[1] // STATE
    per_group = heads // groups
    blocks = tok_rows // STRETCH
    inputs = head_input.reshape(blocks, STRETCH, groups, per_group, HEADP)
    in_maps = input_map.reshape(blocks, STRETCH, groups, STATE)
    out_maps = output_map.reshape(blocks, STRETCH, groups, STATE)
    steps = jnp.transpose(step_size.reshape(heads, blocks, STRETCH), (1, 0, 2))
    rates = jnp.transpose(decays.reshape(heads, blocks, STRETCH), (1, 0, 2))
    within, block_state, accumulated_sums_list, entry = block_term_values(
        inputs, in_maps, out_maps, steps, rates
    )

    def advance(carry, item):
        state, lead = carry
        total, piece = item
        return ((total[..., None, None] * state + piece, total * lead), (state, lead))

    empty_state = jnp.zeros((groups, per_group, HEADP, STATE), jnp.float32)
    unit_decay = jnp.ones((groups, per_group), jnp.float32)
    (local_state, local_decay), (local_entering, leads) = lax.scan(
        advance, (empty_state, unit_decay), (accumulated_sums_list, block_state)
    )
    incoming_decay, incoming = carried_in(
        (local_decay, local_state), "ctx", join_states, (unit_decay, empty_state)
    )
    entering = local_entering + leads[..., None, None] * incoming
    carried = (
        jnp.einsum(
            "kqgn,kgjpn->kqgjp",
            out_maps.astype(jnp.float32),
            entering,
            precision=lax.Precision.HIGHEST,
        )
        * entry
    )
    skip = bypass_scale.reshape(groups, per_group, 1)
    mamba_out = (within + carried + skip * inputs.astype(jnp.float32)).reshape(tok_rows, width)
    gated = mamba_out * jax.nn.silu(gate_input.astype(jnp.float32))
    grouped = gated.reshape(tok_rows, groups, -1)
    factor = lax.rsqrt(jnp.mean(grouped * grouped, axis=-1, keepdims=True) + 1e-05)
    normed = ((grouped * factor).reshape(tok_rows, width) * norm_gain.astype(jnp.float32)).astype(
        jnp.bfloat16
    )
    terms = jnp.dot(
        normed,
        lax.all_gather(out_weight, "ctx", axis=1, tiled=True),
        preferred_element_type=jnp.float32,
    )
    summed = lax.psum_scatter(terms.astype(jnp.bfloat16), "head", scatter_dimension=0, tiled=True)
    return summed


def solution(mesh):
    return jax.shard_map(
        shards,
        mesh=mesh,
        in_specs=(
            P(("group", "ctx"), "head"),
            P(("group", "ctx"), "head"),
            P(("group", "ctx"), "head"),
            P(("group", "ctx"), "head"),
            P("head", ("group", "ctx")),
            P("head", ("group", "ctx")),
            P("head"),
            P("head"),
            P("head", "ctx"),
        ),
        out_specs=P(("group", "ctx", "head"), None),
        check_vma=False,
    )
```

profile of v0, /device:TPU:0, one launch (start us, length us, event | category | flops | bytes accessed | tf_op | source)
XLA Modules:
  0.0 478.2 jit_solution(10169969477722998015)
XLA Ops:
  6.5 0.0 copy-start
  6.5 0.0 all-gather.8.cloned.1.call-start
  6.5 0.9 bitcast_bitcast_fusion
  7.4 1.2 reduce_window_sum.11
  8.6 0.2 slice_reduce_fusion
  8.8 7.1 %reshape.83 = bf16[4,128,2,16,64]{4,3,2,1,0:T(8,128)(2,1)} reshape(bf16[512,2048]{1,0:T(8,128)(2,1)} %param.13) | data formatting | bytes 4194304 | tf_op jit(solution)/shard_map/reshape | solution.py:82
  15.9 0.0 copy-start.5
  15.9 6.5 %copy.27 = bf16[4,128,2,16,64]{1,4,3,2,0:T(8,128)(2,1)} copy(bf16[4,128,2,16,64]{4,3,2,1,0:T(8,128)(2,1)} %reshape.83) | data formatting | bytes 4194304 | tf_op jit(solution)/shard_map/reshape | solution.py:82
  22.4 0.0 copy-done.5
  22.4 0.1 reshape.67
  22.5 0.1 exp.24
  22.6 0.0 copy-done
  22.6 0.1 bitcast_multiply_fusion.2
  22.7 6.1 %fusion.23 = f32[4,2,16,64,256]{4,3,2,1,0:T(8,128)} fusion(bf16[4,128,2,16,64]{1,4,3,2,0:T(8,128)(2,1)} %copy.27, f32[4,128,2,16]{1,3,2,0:T(8,128)S(1)} %bitcast.92, bf16[4,128,2,256,1]{3,2,1,0,4:T(2,128)(2,1)S(1)} %bitcast.89), kind=kOutput, calls=%fused_computation.39 | convolution fusion | flops 540016640 | bytes 11075584 | tf_op jit(solution)/shard_map/ksgjp,ksgn->kgjpn/dot_general | solution.py:50
  28.8 14.3 %while.31 = (s32[]{:T(128)}, f32[2,16,64,256]{3,2,1,0:T(8,128)S(1)}, f32[2,16]{1,0:T(2,128)S(1)}, f32[4,2,16,64,256]{4,3,2,1,0:T(8,128)}, f32[4,2,16]{2,1,0:T(2,...) while((s32[]{:T(128)}, ...), condition=%wide.region_2.3_spmd.clone, body=%wide.region_1.2_spmd.clone.sunk | while | flops 2097251 | bytes 10489078 | solution.py:98
  28.8 1.5 bitcast_dynamic-update-slice_fusion.4
  30.3 2.0 bitcast_add_fusion.2
  32.4 1.5 bitcast_dynamic-update-slice_fusion.4
  33.9 2.0 bitcast_add_fusion.2
  36.0 1.5 bitcast_dynamic-update-slice_fusion.4
  37.5 2.0 bitcast_add_fusion.2
  39.5 1.5 bitcast_dynamic-update-slice_fusion.4
  41.0 2.0 bitcast_add_fusion.2
  43.1 0.0 copy-start.7
  43.1 1.1 convert_element_type.57
  44.2 0.0 all-gather.8.cloned.1.call-update
  44.2 0.0 copy-start.6
  44.2 0.0 all-gather.6.cloned.1.call-start
  44.3 0.7 all-gather.6.cloned.1.call-update
  45.0 0.0 reduce-scatter.2.cloned.1.call-start
  45.1 1.2 reshape.66
  46.2 0.0 copy-done.7
  46.2 0.1 mul.140
  46.3 3.9 copy.32
  50.2 0.0 copy-done.6
  50.3 12.9 %all-gather.2 = bf16[4,2,16]{2,1,0:T(2,128)(2,1)S(1)} all-gather(bf16[1,2,16]{2,1,0:T(2,128)(2,1)S(1)} %convert_bitcast_fusion), channel_id=2, replica_groups=mesh['group'=2,'ctx'=4,'head'=4] {'ctx'}, dimensions={0}, use_global_device_ids=true | all-gather | bytes 320 | tf_op jit(solution)/shard_map/all_gather | solution.py:14
  63.2 1.1 fusion.28
  64.3 63.6 %all-gather.8.cloned.1.call-done = bf16[8,16,64,256]{3,2,1,0:T(8,128)(2,1)} async-done(((bf16[2,16,64,256]{3,2,1,0:T(8,128)(2,1)}), bf16[8,16,64,256]{3,2,1,0:T(8,128)(2,1)}) %all-gather.8.cloned.1.call-update) | async-done | bytes 4194320 | tf_op jit(solution)/shard_map/all_gather | solution.py:14
  127.9 9.2 %while.32 = (s32[]{:T(128)}, f32[2,16,64,256]{3,2,1,0:T(8,128)S(1)}, s32[]{:T(128)}, bf16[4,2,16]{2,1,0:T(2,128)(2,1)S(1)}, bf16[4,2,16,64,256]{4,3,2,1,0:T(8,128)(2,1)}, /*index=5*/s32[]{:T(128)}, s32[]{:T(128)}) while((s32[]{:T(128)}, f32[2,16,64,256]{3,2,1,0:T(8,128)S(1)}, s32[]{:T(128)}, bf16[4,2,16]{2,1,0:T(2,128)(2,1)S(1)}, ...), condition=%wide.region_4.5_spmd.clone, body=%wide.region_3.4_spmd.clone.sunk | while | flops 2621476 | bytes 5243305 | solution.py:31
  127.9 2.2 fusion.40
  130.1 2.2 fusion.40
  132.4 2.2 fusion.40
  134.7 2.4 fusion.40
  137.1 0.0 copy-start.3
  137.1 0.0 copy-start.4
  137.1 8.0 %fusion.2 = f32[4,2,16,64,128]{4,3,2,1,0:T(8,128)S(1)} fusion(f32[4,2,16,64,256]{4,3,2,1,0:T(8,128)} %get-tuple-element.139, f32[2,16,64,256]{3,2,1,0:T(8,128)S(1)} %get-tuple-element.143, f32[4,2,16]{2,1,0:T(2,128)S(1)} %get-tuple-element.140, bf16[4,128,2,256,1]{3,2,1,0,4:T(2,128)(2,1)S(1)} %bitcast.88), kind=kOutput, calls=%fused_computation.9 | convolution fusion | flops 3225419776 | bytes 15204864 | tf_op jit(solution)/shard_map/kqgn,kgjpn->kqgjp/dot_general | solution.py:106
  145.1 0.0 copy-done.3
  145.1 0.0 copy-done.4
  145.1 3.6 fusion.7
  148.8 0.0 copy-start.2
  148.8 3.6 copy.31
  152.4 0.0 copy-done.2
  152.4 1.4 bitcast_reduce_fusion
  153.8 1.7 fusion.13
  155.5 259.2 %all-gather.6.cloned.1.call-done = bf16[2048,4096]{1,0:T(8,128)(2,1)} async-done(((bf16[2048,1024]{1,0:T(8,128)(2,1)}), bf16[2048,4096]{1,0:T(8,128)(2,1)}) %all-gather.6.cloned.1.call-update) | async-done | bytes 16777232 | tf_op jit(solution)/shard_map/all_gather | solution.py:124
  414.8 0.0 copy-start.1
  414.8 14.0 %convolution_convert_fusion = bf16[512,4096]{1,0:T(8,128)(2,1)} fusion(bf16[512,2048]{0,1:T(8,128)(2,1)S(1)} %fusion.13, bf16[2048,4096]{1,0:T(8,128)(2,1)} %all-gather.6.cloned.1.call-done), kind=kOutput, calls=%fused_computation.13 | convolution fusion | flops 8592031744 | bytes 23068672 | tf_op jit(solution)/shard_map/dot_general | solution.py:122
  428.8 0.0 reduce-scatter.2.cloned.1.call-update
  428.8 42.8 %reduce-scatter.2.cloned.1.call-done = bf16[128,4096]{1,0:T(8,128)(2,1)} async-done(((bf16[512,4096]{1,0:T(8,128)(2,1)}), bf16[128,4096]{1,0:T(8,128)(2,1)}) %reduce-scatter.2.cloned.1.call-update) | async-done | bytes 1048592 | tf_op jit(solution)/shard_map/reduce_scatter | solution.py:127
  471.6 0.0 copy-done.1
  (23 shorter events, 0.2 us)
Async XLA Ops:
  6.5 16.1 %copy-start = (f32[32,512]{1,0:T(8,128)S(1)}, f32[32,512]{1,0:T(8,128)}, u32[]{:S(2)}) copy-start(f32[32,512]{1,0:T(8,128)} %param.17) | copy-start | bytes 196612
  6.5 121.3 %all-gather.8.cloned.1.call-start = ((), (), s32[]{:S(2)}) async-start(), calls=%async_computation.3 | async-start | bytes 5242880 | tf_op jit(solution)/shard_map/all_gather | solution.py:14
  15.9 6.5 %copy-start.5 = (bf16[512,512]{1,0:T(8,128)(2,1)S(1)}, bf16[512,512]{1,0:T(8,128)(2,1)}, u32[]{:S(2)}) copy-start(bf16[512,512]{1,0:T(8,128)(2,1)} %param.15) | copy-start | bytes 1572868
  43.1 3.2 copy-start.7
  44.2 6.0 %copy-start.6 = (bf16[2048]{0:T(1024)(128)(2,1)S(1)}, bf16[2048]{0:T(1024)(128)(2,1)}, u32[]{:S(2)}) copy-start(bf16[2048]{0:T(1024)(128)(2,1)} %param.20) | copy-start | bytes 12292
  44.2 370.5 %all-gather.6.cloned.1.call-start = ((), (), s32[]{:S(2)}) async-start(), calls=%async_computation.1 | async-start | bytes 20971520 | tf_op jit(solution)/shard_map/all_gather | solution.py:124
  45.0 426.6 %reduce-scatter.2.cloned.1.call-start = ((), (), s32[]{:S(2)}) async-start(), calls=%async_computation.2 | async-start | bytes 5242880 | tf_op jit(solution)/shard_map/reduce_scatter | solution.py:127
  137.1 8.0 %copy-start.3 = (bf16[4,128,2,16,64]{1,4,3,2,0:T(8,128)(2,1)S(1)}, bf16[4,128,2,16,64]{1,4,3,2,0:T(8,128)(2,1)}, u32[]{:S(2)}) copy-start(bf16[4,128,2,16,64]{1,4,3,2,0:T(8,128)(2,1)} %copy.27) | copy-start | bytes 6291460
  137.1 8.0 %copy-start.4 = (f32[4,2,128,128]{3,2,1,0:T(8,128)S(1)}, f32[4,2,128,128]{3,2,1,0:T(8,128)}, u32[]{:S(2)}) copy-start(f32[4,2,128,128]{3,2,1,0:T(8,128)} %fusion.28) | copy-start | bytes 1572868
  148.8 3.6 copy-start.2
  414.8 56.9 %copy-start.1 = (f32[32,512]{1,0:T(8,128)S(1)}, f32[32,512]{1,0:T(8,128)}, u32[]{:S(2)}) copy-start(f32[32,512]{1,0:T(8,128)} %param.17) | copy-start | bytes 196612
Sparse Core Ops, SparseCore 0:
  44.4 83.4 all-gather.7
  129.4 285.2 all-gather.5
  428.9 42.6 reduce-scatter.1
where the time goes:
time: 479 us; the launch traced here: 478 us
  waiting for transfers between devices  366 us (76%)
  matrix products  32.8 us (7%)
  other arithmetic  28.8 us (6%)
  local copies, waits for them, and re-layouts  23.7 us (5%)
  between operations  13.3 us (3%)
  blocking collectives  12.9 us (3%)
    all_gather x1, waiting for transfers between devices, shards(): lax.all_gather(out_weight, 'ctx', axis=1, tiled=True)  259 us
    all_gather x1, waiting for transfers between devices, carried_in(): lax.all_gather(part.astype(kind), axis)  63.6 us
    reduce_scatter x1, waiting for transfers between devices, shards(): lax.psum_scatter(terms.astype(jnp.bfloat16), 'head', scatter_dimension=0,...  42.8 us
    dot_general x1, matrix products, shards(): jnp.dot(normed, lax.all_gather(out_weight, 'ctx', axis=1, tiled=True), pr...  14 us
    reshape x2, local copies, waits for them, and re-layouts, shards(): inputs = head_input.reshape(blocks, STRETCH, groups, per_group, HEADP)  13.6 us
    all_gather x1, blocking collectives, carried_in(): lax.all_gather(part.astype(kind), axis)  12.9 us
  transfers between devices with their start and end apart: 3, of which 3 were waited for; matrix products, arithmetic and copies ran while one was open for 7% of the time, Pallas kernels for 0%

commit v1 on v0

--- a/solution.py
+++ b/solution.py
@@ -6,6 +6,24 @@
 HEADP = 64
 STATE = 256
 STRETCH = 128
+
+
+def collect(array, axis, dim):
+    ways, here, turn = (lax.axis_size(axis), lax.axis_index(axis), array.shape[dim])
+    shape = [n * ways if d == dim else n for d, n in enumerate(array.shape)]
+    full = lax.dynamic_update_slice_in_dim(
+        jnp.zeros(shape, array.dtype), array, here * turn, axis=dim
+    )
+    going_up = going_down = array
+    for far in range(1, ways // 2 + 1):
+        going_up = lax.ppermute(going_up, axis, [(d, (d + 1) % ways) for d in range(ways)])
+        full = lax.dynamic_update_slice_in_dim(full, going_up, (here - far) % ways * turn, axis=dim)
+        if 2 * far < ways:
+            going_down = lax.ppermute(going_down, axis, [(d, (d - 1) % ways) for d in range(ways)])
+            full = lax.dynamic_update_slice_in_dim(
+                full, going_down, (here + far) % ways * turn, axis=dim
+            )
+    return full
 
 
 def carried_in(shard, axis, combine, identity):
@@ -119,11 +137,7 @@
     normed = ((grouped * factor).reshape(tok_rows, width) * norm_gain.astype(jnp.float32)).astype(
         jnp.bfloat16
     )
-    terms = jnp.dot(
-        normed,
-        lax.all_gather(out_weight, "ctx", axis=1, tiled=True),
-        preferred_element_type=jnp.float32,
-    )
+    terms = jnp.dot(normed, collect(out_weight, "ctx", 1), preferred_element_type=jnp.float32)
     summed = lax.psum_scatter(terms.astype(jnp.bfloat16), "head", scatter_dimension=0, tiled=True)
     return summed
 

time: 479 us -> 472 us (0.985)
  waiting for transfers between devices: 366 us -> 99.3 us
  blocking collectives: 12.9 us -> 246 us
  local copies, waits for them, and re-layouts: 23.7 us -> 45.9 us
  starting transfers between devices: 0.08 us -> 5.35 us
    all_gather x1 -> x0, waiting for transfers between devices: 259 us -> none  [shards(): lax.all_gather(out_weight, 'ctx', axis=1, tiled=True)]
    all_gather x1, blocking collectives: 12.9 us -> 246 us  [carried_in(): lax.all_gather(part.astype(kind), axis)]
    all_gather x1, waiting for transfers between devices: 63.6 us -> 0.01 us  [carried_in(): lax.all_gather(part.astype(kind), axis)]
    ppermute x0 -> x3, waiting for transfers between devices: none -> 56.4 us  [the longest x2 56.4 us: collect(): lax.ppermute(going_up, axis, [(d, (d + 1) % ways) for d in range(ways)])]
    dynamic_update_slice x0 -> x4, local copies, waits for them, and re-layouts: none -> 16.3 us  [the longest x2 9.26 us: collect(): lax.dynamic_update_slice_in_dim(full, going_up, (here - far) % ways * tur...]
    broadcast_in_dim x0 -> x1, local copies, waits for them, and re-layouts: none -> 6.65 us  [collect(): jnp.zeros(shape, array.dtype)]
    ppermute x0 -> x3, starting transfers between devices: none -> 5.31 us  [the longest x2 3.22 us: collect(): lax.ppermute(going_up, axis, [(d, (d + 1) % ways) for d in range(ways)])]
  transfers between devices with their start and end apart: 3 -> 5, of which waited for: 3 -> 2; matrix products, arithmetic and copies ran while one was open for 7% -> 11% of each run, Pallas kernels for 0% -> 0%
where the time goes in v1:
time: 472 us; the launch traced here: 471 us
  blocking collectives  246 us (52%)
  waiting for transfers between devices  99.3 us (21%)
  local copies, waits for them, and re-layouts  45.9 us (10%)
  matrix products  32 us (7%)
  other arithmetic  28.8 us (6%)
  between operations  13.6 us (3%)
  starting transfers between devices  5.35 us (1%)
    all_gather x1, blocking collectives, carried_in(): lax.all_gather(part.astype(kind), axis)  246 us
    ppermute x2, waiting for transfers between devices, collect(): lax.ppermute(going_up, axis, [(d, (d + 1) % ways) for d in range(ways)])  56.4 us
    reduce_scatter x1, waiting for transfers between devices, shards(): lax.psum_scatter(terms.astype(jnp.bfloat16), 'head', scatter_dimension=0,...  42.9 us
    dot_general x1, matrix products, shards(): jnp.dot(normed, collect(out_weight, 'ctx', 1), preferred_element_type=jnp...  14 us
    reshape x2, local copies, waits for them, and re-layouts, shards(): inputs = head_input.reshape(blocks, STRETCH, groups, per_group, HEADP)  13.7 us
  transfers between devices with their start and end apart: 5, of which 2 were waited for; matrix products, arithmetic and copies ran while one was open for 11% of the time, Pallas kernels for 0%

profile of v1, /device:TPU:0, one launch (start us, length us, event | category | flops | bytes accessed | tf_op | source)
XLA Modules:
  0.0 471.3 jit_solution(1724016057343705613)
XLA Ops:
  6.5 0.0 copy-start
  6.5 0.0 all-gather.5.cloned.1.call-start
  6.5 7.1 %reshape.83 = bf16[4,128,2,16,64]{4,3,2,1,0:T(8,128)(2,1)} reshape(bf16[512,2048]{1,0:T(8,128)(2,1)} %param.13) | data formatting | bytes 4194304 | tf_op jit(solution)/shard_map/reshape | solution.py:100
  13.6 6.6 %copy.27 = bf16[4,128,2,16,64]{1,4,3,2,0:T(8,128)(2,1)} copy(bf16[4,128,2,16,64]{4,3,2,1,0:T(8,128)(2,1)} %reshape.83) | data formatting | bytes 4194304 | tf_op jit(solution)/shard_map/reshape | solution.py:100
  20.2 0.0 copy-done.7
  20.3 1.2 reduce_window_sum.11
  21.4 0.2 slice_reduce_fusion
  21.6 0.1 exp.24
  21.7 0.0 copy-done.6
  21.7 0.1 reshape.67
  21.8 0.0 copy-done
  21.8 0.1 bitcast_multiply_fusion.2
  21.9 6.1 %fusion.23 = f32[4,2,16,64,256]{4,3,2,1,0:T(8,128)} fusion(bf16[4,128,2,16,64]{1,4,3,2,0:T(8,128)(2,1)} %copy.27, f32[4,128,2,16]{1,3,2,0:T(8,128)S(1)} %bitcast.92, bf16[4,128,2,256,1]{3,2,1,0,4:T(2,128)(2,1)S(1)} %bitcast.89), kind=kOutput, calls=%fused_computation.39 | convolution fusion | flops 540016640 | bytes 11075584 | tf_op jit(solution)/shard_map/ksgjp,ksgn->kgjpn/dot_general | solution.py:68
  28.0 14.5 %while.31 = (s32[]{:T(128)}, f32[2,16,64,256]{3,2,1,0:T(8,128)S(1)}, f32[2,16]{1,0:T(2,128)S(1)}, f32[4,2,16,64,256]{4,3,2,1,0:T(8,128)}, f32[4,2,16]{2,1,0:T(2,...) while((s32[]{:T(128)}, ...), condition=%wide.region_2.3_spmd.clone, body=%wide.region_1.2_spmd.clone.sunk | while | flops 2097251 | bytes 10488578 | solution.py:116
  28.0 1.6 bitcast_dynamic-update-slice_fusion.4
  29.6 2.0 bitcast_add_fusion.2
  31.6 1.5 bitcast_dynamic-update-slice_fusion.4
  33.2 2.0 bitcast_add_fusion.2
  35.2 1.6 bitcast_dynamic-update-slice_fusion.4
  36.8 2.0 bitcast_add_fusion.2
  38.9 1.6 bitcast_dynamic-update-slice_fusion.4
  40.5 2.0 bitcast_add_fusion.2
  42.5 0.0 copy-start.8
  42.5 0.0 copy-start.9
  42.5 1.1 convert_element_type.57
  43.6 0.0 all-gather.5.cloned.1.call-update
  43.7 0.0 reduce-scatter.2.cloned.1.call-start
  43.7 3.1 collective-permute-start
  46.8 2.1 collective-permute-start.1
  48.9 0.0 copy-done.8
  48.9 3.9 copy.32
  52.8 1.2 reshape.66
  54.0 0.0 copy-done.9
  54.0 0.1 mul.152
  54.1 246.2 %all-gather.2 = bf16[4,2,16]{2,1,0:T(2,128)(2,1)S(1)} all-gather(bf16[1,2,16]{2,1,0:T(2,128)(2,1)S(1)} %convert_bitcast_fusion), channel_id=2, replica_groups=mesh['group'=2,'ctx'=4,'head'=4] {'ctx'}, dimensions={0}, use_global_device_ids=true | all-gather | bytes 320 | tf_op jit(solution)/shard_map/all_gather | solution.py:32
  300.3 1.1 fusion.28
  301.4 6.6 %broadcast_in_dim.54 = bf16[2048,4096]{1,0:T(8,128)(2,1)} broadcast(bf16[]{:T(256)} %constant.84.clone.1), dimensions={} | broadcast | bytes 16777218 | tf_op jit(solution)/shard_map/broadcast_in_dim | solution.py:15
  308.1 0.0 copy-done.4
  308.1 2.5 constant_dynamic-update-slice_fusion.3
  310.5 0.0 collective-permute-done
  310.6 0.1 collective-permute-start.2
  310.7 4.7 constant_dynamic-update-slice_fusion.2
  315.4 0.0 collective-permute-done.1
  315.4 4.6 constant_dynamic-update-slice_fusion.1
  320.0 9.0 %while.32 = (s32[]{:T(128)}, f32[2,16,64,256]{3,2,1,0:T(8,128)S(1)}, s32[]{:T(128)}, bf16[4,2,16]{2,1,0:T(2,128)(2,1)S(1)}, bf16[4,2,16,64,256]{4,3,2,1,0:T(8,128)(2,1)}, /*index=5*/s32[]{:T(128)}, s32[]{:T(128)}) while((s32[]{:T(128)}, f32[2,16,64,256]{3,2,1,0:T(8,128)S(1)}, s32[]{:T(128)}, bf16[4,2,16]{2,1,0:T(2,128)(2,1)S(1)}, ...), condition=%wide.region_4.5_spmd.clone, body=%wide.region_3.4_spmd.clone.sunk | while | flops 2621476 | bytes 5243313 | solution.py:49
  320.0 2.2 fusion.40
  322.2 2.2 fusion.40
  324.5 2.2 fusion.40
  326.8 2.2 fusion.40
  329.0 0.0 copy-start.3
  329.0 0.0 copy-start.5
  329.0 7.2 %fusion.2 = f32[4,2,16,64,128]{4,3,2,1,0:T(8,128)S(1)} fusion(f32[4,2,16,64,256]{4,3,2,1,0:T(8,128)} %get-tuple-element.139, f32[2,16,64,256]{3,2,1,0:T(8,128)S(1)} %get-tuple-element.143, f32[4,2,16]{2,1,0:T(2,128)S(1)} %get-tuple-element.140, bf16[4,128,2,256,1]{3,2,1,0,4:T(2,128)(2,1)S(1)} %bitcast.88), kind=kOutput, calls=%fused_computation.9 | convolution fusion | flops 3225419776 | bytes 15204864 | tf_op jit(solution)/shard_map/kqgn,kgjpn->kqgjp/dot_general | solution.py:124
  336.2 0.0 copy-done.3
  336.2 0.0 copy-done.5
  336.2 3.6 fusion.7
  339.9 0.0 copy-start.2
  339.9 3.6 copy.31
  343.5 1.4 bitcast_reduce_fusion
  344.9 1.7 fusion.13
  346.6 56.4 %collective-permute-done.2 = bf16[2048,1024]{1,0:T(8,128)(2,1)} collective-permute-done((bf16[2048,1024]{1,0:T(8,128)(2,1)}, bf16[2048,1024]{1,0:T(8,128)(2,1)}, u32[]{:S(2)}, u32[]{:S(2)}) %collective-permute-start.2) | collective-permute-done | bytes 4194336 | tf_op jit(solution)/shard_map/ppermute | solution.py:19
  403.0 4.6 constant_dynamic-update-slice_fusion
  407.6 14.0 %convolution_convert_fusion = bf16[512,4096]{1,0:T(8,128)(2,1)} fusion(bf16[512,2048]{0,1:T(8,128)(2,1)S(1)} %fusion.13, bf16[2048,4096]{1,0:T(8,128)(2,1)} %constant_dynamic-update-slice_fusion), kind=kOutput, calls=%fused_computation.13 | convolution fusion | flops 8592031744 | bytes 23068672 | tf_op jit(solution)/shard_map/dot_general | solution.py:140
  421.6 0.0 reduce-scatter.2.cloned.1.call-update
  421.6 42.9 %reduce-scatter.2.cloned.1.call-done = bf16[128,4096]{1,0:T(8,128)(2,1)} async-done(((bf16[512,4096]{1,0:T(8,128)(2,1)}), bf16[128,4096]{1,0:T(8,128)(2,1)}) %reduce-scatter.2.cloned.1.call-update) | async-done | bytes 1048592 | tf_op jit(solution)/shard_map/reduce_scatter | solution.py:141
  (31 shorter events, 0.2 us)
Async XLA Ops:
  6.5 15.3 %copy-start = (f32[32,512]{1,0:T(8,128)S(1)}, f32[32,512]{1,0:T(8,128)}, u32[]{:S(2)}) copy-start(f32[32,512]{1,0:T(8,128)} %param.17) | copy-start | bytes 196612
  6.5 313.4 %all-gather.5.cloned.1.call-start = ((), (), s32[]{:S(2)}) async-start(), calls=%async_computation.2 | async-start | bytes 5242880 | tf_op jit(solution)/shard_map/all_gather | solution.py:32
  13.6 6.6 %copy-start.7 = (f32[32,512]{1,0:T(8,128)S(1)}, f32[32,512]{1,0:T(8,128)}, u32[]{:S(2)}) copy-start(f32[32,512]{1,0:T(8,128)} %param.18) | copy-start | bytes 196612
  13.6 8.0 %copy-start.6 = (bf16[512,512]{1,0:T(8,128)(2,1)S(1)}, bf16[512,512]{1,0:T(8,128)(2,1)}, u32[]{:S(2)}) copy-start(bf16[512,512]{1,0:T(8,128)(2,1)} %param.15) | copy-start | bytes 1572868
  42.5 6.4 %copy-start.8 = (bf16[2048]{0:T(1024)(128)(2,1)S(1)}, bf16[2048]{0:T(1024)(128)(2,1)}, u32[]{:S(2)}) copy-start(bf16[2048]{0:T(1024)(128)(2,1)} %param.20) | copy-start | bytes 12292
  42.5 11.5 %copy-start.9 = (f32[32]{0:T(128)S(1)}, f32[32]{0:T(128)}, u32[]{:S(2)}) copy-start(f32[32]{0:T(128)} %param.19) | copy-start | bytes 388
  43.7 420.8 %reduce-scatter.2.cloned.1.call-start = ((), (), s32[]{:S(2)}) async-start(), calls=%async_computation.1 | async-start | bytes 5242880 | tf_op jit(solution)/shard_map/reduce_scatter | solution.py:141
  43.7 266.8 %collective-permute-start = (bf16[2048,1024]{1,0:T(8,128)(2,1)}, bf16[2048,1024]{1,0:T(8,128)(2,1)}, u32[]{:S(2)}, u32[]{:S(2)}) collective-permute-start(bf16[2048,1024]{1,0:T(8,128)(2,1)} %param.21), channel_id=1, source_target_pairs={{0,4},{4,8},{8,12},{12,0},{1,5},{5,9},{9,13},{13,1},{2,6},{6,10},{... | collective-permute-start | bytes 12582920 | tf_op jit(solution)/shard_map/ppermute | solution.py:19
  46.8 268.6 %collective-permute-start.1 = (bf16[2048,1024]{1,0:T(8,128)(2,1)}, bf16[2048,1024]{1,0:T(8,128)(2,1)}, u32[]{:S(2)}, u32[]{:S(2)}) collective-permute-start(bf16[2048,1024]{1,0:T(8,128)(2,1)} %param.21), channel_id=1, source_target_pairs={{0,12},{4,0},{8,4},{12,8},{1,13},{5,1},{9,5},{13,9},{2,14},{6,2},{... | collective-permute-start | bytes 12582920 | tf_op jit(solution)/shard_map/ppermute | solution.py:22
  301.4 6.7 %copy-start.4 = (bf16[2048,1024]{1,0:T(8,128)(2,1)S(1)}, bf16[2048,1024]{1,0:T(8,128)(2,1)}, u32[]{:S(2)}) copy-start(bf16[2048,1024]{1,0:T(8,128)(2,1)} %param.21) | copy-start | bytes 12582916
  310.6 92.4 %collective-permute-start.2 = (bf16[2048,1024]{1,0:T(8,128)(2,1)}, bf16[2048,1024]{1,0:T(8,128)(2,1)}, u32[]{:S(2)}, u32[]{:S(2)}) collective-permute-start(bf16[2048,1024]{1,0:T(8,128)(2,1)} %collective-permute-done), channel_id=1, source_target_pairs={{0,4},{4,8},{8,12},{12,0},{1,5},{5,9},{9,13},{13,1},{2,6},{6,10},{... | collective-permute-start | bytes 12582920 | tf_op jit(solution)/shard_map/ppermute | solution.py:19
  329.0 7.2 %copy-start.3 = (bf16[4,128,2,16,64]{1,4,3,2,0:T(8,128)(2,1)S(1)}, bf16[4,128,2,16,64]{1,4,3,2,0:T(8,128)(2,1)}, u32[]{:S(2)}) copy-start(bf16[4,128,2,16,64]{1,4,3,2,0:T(8,128)(2,1)} %copy.27) | copy-start | bytes 6291460
  329.0 7.2 %copy-start.5 = (f32[4,2,128,128]{3,2,1,0:T(8,128)S(1)}, f32[4,2,128,128]{3,2,1,0:T(8,128)}, u32[]{:S(2)}) copy-start(f32[4,2,128,128]{3,2,1,0:T(8,128)} %fusion.28) | copy-start | bytes 1572868
  339.9 3.6 copy-start.2
  407.6 56.9 %copy-start.1 = (f32[32,512]{1,0:T(8,128)S(1)}, f32[32,512]{1,0:T(8,128)}, u32[]{:S(2)}) copy-start(f32[32,512]{1,0:T(8,128)} %param.17) | copy-start | bytes 196612
Sparse Core Ops, SparseCore 0:
  43.8 197.4 all-gather.4
  421.7 42.7 reduce-scatter.1
